TPU v7x, 32 devices: a whole 2x2x4 slice. The times are simulated.
32 devices in a mesh: group: 2 (over y), tm: 8 (over z, core), pix: 2 (over x), sub: 1.
Axes of the slice: x: 2, y: 2, z: 4, core: 2. Of those that a mesh axis runs over, the one named last changes fastest.
Arguments:
- anomaly: bfloat16 [512, 65536], P('tm', ('group', 'pix', 'sub')), parts along dimension 1, may hold values from -6 to 6
- offsets: int32 [32], replicated, may hold values from 0 to 256, as said below
- taper_index: int32 [32], replicated, may hold values from 0 to 3
Outputs:
- spectral_gram: float32 [256, 64, 64], P(('group', 'tm')), parts along dimension 0
- leading_energy: float32 [256], P(('group', 'tm')), parts along dimension 0
There are 2 independent parts, one for each index of `group`. A program takes and returns all parts, laid end to end along the dimension named above; an argument that names none is the same for every part. Nothing has to cross between parts.
Inputs may be any that keep to these rules, and one draw needn't show every extreme that they name: `offsets`: block starts never fall; the first block starts at day 0 and the last at day 512 - 256.
All inputs are finite; a program needn't handle non-finite values.
Results may differ from a plain program's by a relative error of at most 0.0034.
Values may be sent and summed in bfloat16 or wider, within the bound.
A program may use at most 128 MiB of HBM per device.

v0:
```python
import math
import jax
import jax.numpy as jnp
from jax import lax
from jax.sharding import PartitionSpec as P

NFFT = 256
NB = 32
POWER = 8
NF = 128
power_eps = 1e-06


def window_rows(taper_index, length):
    steps_t = jnp.arange(length, dtype=jnp.float32)
    phase = steps_t * (2.0 * math.pi / length)
    center = (steps_t + 0.5) * (math.pi / length)
    hann = jnp.sin(center) ** 2
    hamming = 0.54 - 0.46 * jnp.cos(phase)
    blackman = 0.42 - 0.5 * jnp.cos(phase) + 0.08 * jnp.cos(2.0 * phase)
    sine_win = jnp.sin(center)
    table_rows = jnp.stack([hann, hamming, blackman, sine_win])
    chosen = jnp.zeros((taper_index.shape[0], length), jnp.float32)
    for which in range(4):
        chosen = chosen + jnp.where(
            taper_index[:, None] == which, table_rows[which][None, :], jnp.float32(0.0)
        )
    return chosen


def dft_table(length, kept):
    freqs = jnp.arange(kept, dtype=jnp.int32)
    times = jnp.arange(length, dtype=jnp.int32)
    product = freqs[:, None] * times[None, :] % length
    angle = product.astype(jnp.float32) * (2.0 * math.pi / length)
    return jnp.stack([jnp.cos(angle), -jnp.sin(angle)]).astype(jnp.bfloat16)


def local_gram(spectra):
    stacked = spectra.reshape(2 * spectra.shape[1], spectra.shape[2], spectra.shape[3])
    return jnp.einsum("ifp,jfp->fij", stacked, stacked, preferred_element_type=jnp.float32)


def shards(anomaly, offsets, taper_index):
    series = lax.all_to_all(anomaly, "tm", split_axis=1, concat_axis=0, tiled=True)
    windows = window_rows(taper_index, NFFT)
    energy = 1.0 / jnp.sqrt(jnp.sum(windows * windows, axis=1))
    transform = dft_table(NFFT, NF)
    width_here = series.shape[1]
    per_group = 8
    gram_width = 2 * NB

    def fill_group(position, buffer):
        first_block = position * per_group
        starts = lax.dynamic_slice_in_dim(offsets, first_block, per_group, 0)
        shapes = lax.dynamic_slice_in_dim(windows, first_block, per_group, 0)
        scales = lax.dynamic_slice_in_dim(energy, first_block, per_group, 0)
        segments = jax.vmap(lambda first_day: lax.dynamic_slice_in_dim(series, first_day, NFFT, 0))(
            starts
        )
        windowed = (segments * shapes[:, :, None]).astype(jnp.bfloat16)
        spectra = jnp.einsum(
            "rkt,btp->rbkp", transform, windowed, preferred_element_type=jnp.float32
        )
        spectra = (spectra * scales[None, :, None, None]).astype(jnp.bfloat16)
        return lax.dynamic_update_slice_in_dim(buffer, spectra, first_block, 1)

    empty = jnp.zeros((2, NB, NF, width_here), jnp.bfloat16)
    spectra = lax.fori_loop(0, NB // per_group, fill_group, empty)
    received = lax.all_to_all(spectra, "tm", split_axis=2, concat_axis=3, tiled=True)
    partial_value = local_gram(received)
    summed = lax.psum(partial_value, ("pix", "sub"))
    total_pixels = anomaly.shape[1] * lax.axis_size(("pix", "sub"))
    spectral_gram = summed / total_pixels
    vector = jnp.ones((spectral_gram.shape[0], gram_width), jnp.float32)
    for _ in range(POWER):
        applied = jnp.einsum("fij,fj->fi", spectral_gram, vector, precision=lax.Precision.HIGHEST)
        vector = applied / jnp.sqrt(jnp.mean(applied * applied, axis=1, keepdims=True) + power_eps)
    applied = jnp.einsum("fij,fj->fi", spectral_gram, vector, precision=lax.Precision.HIGHEST)
    leading_energy = jnp.sqrt(jnp.mean(applied * applied, axis=1))
    return (spectral_gram, leading_energy)


def solution(mesh):
    placed = (P("tm", ("group", "pix", "sub")), P(), P())
    return jax.shard_map(
        shards,
        mesh=mesh,
        in_specs=placed,
        out_specs=(P(("group", "tm"), None, None), P(("group", "tm"))),
        check_vma=False,
    )
```

profile of v0, /device:TPU:0, one launch (start us, length us, event | category | flops | bytes accessed | tf_op | source)
XLA Modules:
  0.0 1170.2 jit_solution(9330474396484308255)
XLA Ops:
  7.2 3.2 copy.48
  10.4 6.3 all-to-all-start
  18.3 47.5 %all-to-all-done = bf16[64,8,2048]{2,0,1:T(8,128)(2,1)S(1)} async-done(((bf16[64,8,2048]{2,0,1:T(8,128)(2,1)}), bf16[64,8,2048]{2,0,1:T(8,128)(2,1)S(1)}, u32[]{:S(2)}, u32[]{:S(2)}) %all-to-all-start) | async-done | bytes 2097184 | tf_op jit(solution)/shard_map/all_to_all | solution.py:45
  65.8 11.0 broadcast_in_dim.86.clone
  76.7 208.3 %while.16 = (s32[]{:T(128)}, bf16[2,32,128,2048]{3,1,0,2:T(8,128)(2,1)}, s32[32]{0:T(128)S(1)}, bf16[512,2048]{1,0:T(8,128)(2,1)S(1)}, f32[32,256]{1,0:T(8,128)S...) while((s32[]{:T(128)}, ...), condition=%wide.region_2.3_spmd, body=%wide.region_1.2_spmd.sunk | while | flops 2168455168 | bytes 52586048 | solution.py:69
  76.8 19.1 %while.17 = (s32[]{:T(128)}, bf16[512,2048]{1,0:T(8,128)(2,1)S(1)}, s32[8,2]{0,1:T(2,128)S(1)}, bf16[8,256,2048]{2,1,0:T(8,128)(2,1)}, s32[]{:T(128)}) while((s32[]{:T(128)}, bf16[512,2048]{1,0:T(8,128)(2,1)S(1)}, s32[8,2]{0,1:T(2,128)S(1)}, bf16[8,256,2048]{2,1,0:T(8,128)(2,1)}, s32[]{:T(128)}) %tuple.54), condition=%wide.while_cond, body=%wide.while_body.sunk | while | flops 2 | bytes 2098265 | solution.py:58
  79.7 1.9 bitcast_dynamic-update-slice_fusion.2
  89.3 1.8 bitcast_dynamic-update-slice_fusion.2
  96.0 12.1 %fusion.53 = bf16[2,8,128,2048]{2,3,0,1:T(8,128)(2,1)} fusion(f32[8]{0:T(128)S(1)} %dynamic_slice.28, bf16[8,256,2048]{2,1,0:T(8,128)(2,1)} %get-tuple-element.242, f32[8,256]{1,0:T(8,128)S(1)} %constant_dynamic-slice_fusion.4, bf16[2,128,256]{2,1,0:T(8,128)(2,1)S(1)} %get-tuple-element.292), kind=kOutput, calls=%fused_computation.6.clone.1 | convolution fusion | flops 2168455168 | bytes 16916512 | tf_op jit(solution)/shard_map/while/body/eval_jaxpr/rkt,btp->rbkp/dot_general | solution.py:62
  108.0 12.6 %copy.50 = bf16[2,8,128,2048]{3,1,0,2:T(8,128)(2,1)} copy(bf16[2,8,128,2048]{2,3,0,1:T(8,128)(2,1)} %fusion.53) | data formatting | bytes 16777216 | tf_op jit(solution)/shard_map/while/body/eval_jaxpr/dynamic_update_slice | solution.py:66
  120.6 8.2 constant_dynamic-update-slice_fusion.2
  128.9 19.1 %while.17 = (s32[]{:T(128)}, bf16[512,2048]{1,0:T(8,128)(2,1)S(1)}, s32[8,2]{0,1:T(2,128)S(1)}, bf16[8,256,2048]{2,1,0:T(8,128)(2,1)}, s32[]{:T(128)}) while((s32[]{:T(128)}, bf16[512,2048]{1,0:T(8,128)(2,1)S(1)}, s32[8,2]{0,1:T(2,128)S(1)}, bf16[8,256,2048]{2,1,0:T(8,128)(2,1)}, s32[]{:T(128)}) %tuple.54), condition=%wide.while_cond, body=%wide.while_body.sunk | while | flops 2 | bytes 2098265 | solution.py:58
  131.8 1.9 bitcast_dynamic-update-slice_fusion.2
  141.3 1.8 bitcast_dynamic-update-slice_fusion.2
  148.0 12.1 %fusion.53 = bf16[2,8,128,2048]{2,3,0,1:T(8,128)(2,1)} fusion(f32[8]{0:T(128)S(1)} %dynamic_slice.28, bf16[8,256,2048]{2,1,0:T(8,128)(2,1)} %get-tuple-element.242, f32[8,256]{1,0:T(8,128)S(1)} %constant_dynamic-slice_fusion.4, bf16[2,128,256]{2,1,0:T(8,128)(2,1)S(1)} %get-tuple-element.292), kind=kOutput, calls=%fused_computation.6.clone.1 | convolution fusion | flops 2168455168 | bytes 16916512 | tf_op jit(solution)/shard_map/while/body/eval_jaxpr/rkt,btp->rbkp/dot_general | solution.py:62
  160.1 12.6 %copy.50 = bf16[2,8,128,2048]{3,1,0,2:T(8,128)(2,1)} copy(bf16[2,8,128,2048]{2,3,0,1:T(8,128)(2,1)} %fusion.53) | data formatting | bytes 16777216 | tf_op jit(solution)/shard_map/while/body/eval_jaxpr/dynamic_update_slice | solution.py:66
  172.6 8.2 constant_dynamic-update-slice_fusion.2
  181.0 19.1 %while.17 = (s32[]{:T(128)}, bf16[512,2048]{1,0:T(8,128)(2,1)S(1)}, s32[8,2]{0,1:T(2,128)S(1)}, bf16[8,256,2048]{2,1,0:T(8,128)(2,1)}, s32[]{:T(128)}) while((s32[]{:T(128)}, bf16[512,2048]{1,0:T(8,128)(2,1)S(1)}, s32[8,2]{0,1:T(2,128)S(1)}, bf16[8,256,2048]{2,1,0:T(8,128)(2,1)}, s32[]{:T(128)}) %tuple.54), condition=%wide.while_cond, body=%wide.while_body.sunk | while | flops 2 | bytes 2098265 | solution.py:58
  183.9 1.9 bitcast_dynamic-update-slice_fusion.2
  200.1 12.1 %fusion.53 = bf16[2,8,128,2048]{2,3,0,1:T(8,128)(2,1)} fusion(f32[8]{0:T(128)S(1)} %dynamic_slice.28, bf16[8,256,2048]{2,1,0:T(8,128)(2,1)} %get-tuple-element.242, f32[8,256]{1,0:T(8,128)S(1)} %constant_dynamic-slice_fusion.4, bf16[2,128,256]{2,1,0:T(8,128)(2,1)S(1)} %get-tuple-element.292), kind=kOutput, calls=%fused_computation.6.clone.1 | convolution fusion | flops 2168455168 | bytes 16916512 | tf_op jit(solution)/shard_map/while/body/eval_jaxpr/rkt,btp->rbkp/dot_general | solution.py:62
  212.2 12.6 %copy.50 = bf16[2,8,128,2048]{3,1,0,2:T(8,128)(2,1)} copy(bf16[2,8,128,2048]{2,3,0,1:T(8,128)(2,1)} %fusion.53) | data formatting | bytes 16777216 | tf_op jit(solution)/shard_map/while/body/eval_jaxpr/dynamic_update_slice | solution.py:66
  224.7 8.2 constant_dynamic-update-slice_fusion.2
  233.0 19.1 %while.17 = (s32[]{:T(128)}, bf16[512,2048]{1,0:T(8,128)(2,1)S(1)}, s32[8,2]{0,1:T(2,128)S(1)}, bf16[8,256,2048]{2,1,0:T(8,128)(2,1)}, s32[]{:T(128)}) while((s32[]{:T(128)}, bf16[512,2048]{1,0:T(8,128)(2,1)S(1)}, s32[8,2]{0,1:T(2,128)S(1)}, bf16[8,256,2048]{2,1,0:T(8,128)(2,1)}, s32[]{:T(128)}) %tuple.54), condition=%wide.while_cond, body=%wide.while_body.sunk | while | flops 2 | bytes 2098265 | solution.py:58
  236.0 1.9 bitcast_dynamic-update-slice_fusion.2
  252.2 12.1 %fusion.53 = bf16[2,8,128,2048]{2,3,0,1:T(8,128)(2,1)} fusion(f32[8]{0:T(128)S(1)} %dynamic_slice.28, bf16[8,256,2048]{2,1,0:T(8,128)(2,1)} %get-tuple-element.242, f32[8,256]{1,0:T(8,128)S(1)} %constant_dynamic-slice_fusion.4, bf16[2,128,256]{2,1,0:T(8,128)(2,1)S(1)} %get-tuple-element.292), kind=kOutput, calls=%fused_computation.6.clone.1 | convolution fusion | flops 2168455168 | bytes 16916512 | tf_op jit(solution)/shard_map/while/body/eval_jaxpr/rkt,btp->rbkp/dot_general | solution.py:62
  264.2 12.6 %copy.50 = bf16[2,8,128,2048]{3,1,0,2:T(8,128)(2,1)} copy(bf16[2,8,128,2048]{2,3,0,1:T(8,128)(2,1)} %fusion.53) | data formatting | bytes 16777216 | tf_op jit(solution)/shard_map/while/body/eval_jaxpr/dynamic_update_slice | solution.py:66
  276.8 8.2 constant_dynamic-update-slice_fusion.2
  285.0 736.0 %all_to_all.34 = bf16[2,32,128,2048]{3,1,0,2:T(8,128)(2,1)} all-to-all(bf16[2,32,128,2048]{3,1,0,2:T(8,128)(2,1)} %get-tuple-element.126), channel_id=1, replica_groups=mesh['group'=2,'tm'=8,'pix'=2,'sub'=1] {'tm'}, dimensions={2} | all-to-all | bytes 67108864 | tf_op jit(solution)/shard_map/all_to_all | solution.py:70
  1021.0 30.0 %copy.21 = bf16[2,32,16,8,2048]{4,3,1,0,2:T(8,128)(2,1)} copy(bf16[2,32,16,8,2048]{4,1,0,2,3:T(8,128)(2,1)} %bitcast.107) | data formatting | bytes 67108864 | tf_op jit(solution)/shard_map/all_to_all | solution.py:70
  1051.0 49.9 %reshape.182 = bf16[64,16,16384]{2,0,1:T(8,128)(2,1)} reshape(bf16[2,32,16,8,2048]{4,3,1,0,2:T(8,128)(2,1)} %copy.21) | data formatting | bytes 67108864 | tf_op jit(solution)/shard_map/reshape | solution.py:40
  1100.9 23.5 %fusion.16 = f32[16,64,64]{2,1,0:T(8,128)} fusion(bf16[64,16,16384]{2,0,1:T(8,128)(2,1)} %reshape.182), kind=kOutput, calls=%fused_computation.64 | convolution fusion | flops 2147483648 | bytes 33816576 | tf_op jit(solution)/shard_map/ifp,jfp->fij/dot_general | solution.py:41
  1124.4 27.1 %all-reduce.3.cloned.1.call-done = f32[16,64,64]{2,1,0:T(8,128)} async-done(((f32[16,64,64]{2,1,0:T(8,128)}), f32[16,64,64]{2,1,0:T(8,128)}) %all-reduce.3.cloned.1.call-update) | async-done | bytes 262160 | tf_op jit(solution)/shard_map/psum | solution.py:72
  (160 shorter events, 79.1 us)
Async XLA Ops:
  10.4 55.4 %all-to-all-start = ((bf16[64,8,2048]{2,0,1:T(8,128)(2,1)}), bf16[64,8,2048]{2,0,1:T(8,128)(2,1)S(1)}, u32[]{:S(2)}, u32[]{:S(2)}) async-start(bf16[64,8,2048]{2,0,1:T(8,128)(2,1)} %bitcast.108), calls=%async_computation | async-start | bytes 4194304 | tf_op jit(solution)/shard_map/all_to_all | solution.py:45
  16.7 1134.8 %all-reduce.3.cloned.1.call-start = ((), (), s32[]{:S(2)}) async-start(), calls=%async_computation.2 | async-start | bytes 1048576 | tf_op jit(solution)/shard_map/psum | solution.py:72
  65.7 11.0 copy-start.1
  1152.6 10.8 copy-start
Sparse Core Ops, SparseCore 0:
  1124.5 26.9 all-reduce.2
where the time goes:
time: 1170 us
  blocking collectives  736 us (63%)
  local copies, waits for them, and re-layouts  254 us (22%)
  matrix products  80.2 us (7%)
  waiting for transfers between devices  74.6 us (6%)
  between operations  14.2 us (1%)
    all_to_all x1, blocking collectives, shards(): lax.all_to_all(spectra, 'tm', split_axis=2, concat_axis=3, tiled=True)  736 us
    dynamic_update_slice x8, local copies, waits for them, and re-layouts, fill_group(): return lax.dynamic_update_slice_in_dim(buffer, spectra, first_block, 1)  83.1 us
    gather x96, local copies, waits for them, and re-layouts  76.2 us
    reshape x1, local copies, waits for them, and re-layouts, local_gram(): spectra.reshape(2 * spectra.shape[1], spectra.shape[2], spectra.shape[3])  49.9 us
    dot_general x4, matrix products, fill_group(): jnp.einsum('rkt,btp->rbkp', transform, windowed, preferred_element_type=j...  48.2 us
    all_to_all x1, waiting for transfers between devices, shards(): lax.all_to_all(anomaly, 'tm', split_axis=1, concat_axis=0, tiled=True)  47.5 us
    all_to_all x1, local copies, waits for them, and re-layouts, shards(): lax.all_to_all(spectra, 'tm', split_axis=2, concat_axis=3, tiled=True)  30 us
    psum x1, waiting for transfers between devices, shards(): summed = lax.psum(partial_value, ('pix', 'sub'))  27.1 us
  transfers between devices with their start and end apart: 2, of which 2 were waited for; matrix products, arithmetic and copies ran while one was open for 0% of the time, Pallas kernels for 0%

commit v1 on v0

--- a/solution.py
+++ b/solution.py
@@ -69,7 +69,7 @@
     spectra = lax.fori_loop(0, NB // per_group, fill_group, empty)
     received = lax.all_to_all(spectra, "tm", split_axis=2, concat_axis=3, tiled=True)
     partial_value = local_gram(received)
-    summed = lax.psum(partial_value, ("pix", "sub"))
+    summed = lax.psum(lax.psum(partial_value, "pix"), "sub")
     total_pixels = anomaly.shape[1] * lax.axis_size(("pix", "sub"))
     spectral_gram = summed / total_pixels
     vector = jnp.ones((spectral_gram.shape[0], gram_width), jnp.float32)

time: 1170 us -> 1170 us (level)
  no operation moved by 1% of the time
where the time goes in v1:
time: 1170 us
  blocking collectives  736 us (63%)
  local copies, waits for them, and re-layouts  254 us (22%)
  matrix products  80.2 us (7%)
  waiting for transfers between devices  74.6 us (6%)
  between operations  14.2 us (1%)
    all_to_all x1, blocking collectives, shards(): lax.all_to_all(spectra, 'tm', split_axis=2, concat_axis=3, tiled=True)  736 us
    dynamic_update_slice x8, local copies, waits for them, and re-layouts, fill_group(): return lax.dynamic_update_slice_in_dim(buffer, spectra, first_block, 1)  83.1 us
    gather x96, local copies, waits for them, and re-layouts  76.2 us
    reshape x1, local copies, waits for them, and re-layouts, local_gram(): spectra.reshape(2 * spectra.shape[1], spectra.shape[2], spectra.shape[3])  49.9 us
    dot_general x4, matrix products, fill_group(): jnp.einsum('rkt,btp->rbkp', transform, windowed, preferred_element_type=j...  48.2 us
    all_to_all x1, waiting for transfers between devices, shards(): lax.all_to_all(anomaly, 'tm', split_axis=1, concat_axis=0, tiled=True)  47.5 us
    all_to_all x1, local copies, waits for them, and re-layouts, shards(): lax.all_to_all(spectra, 'tm', split_axis=2, concat_axis=3, tiled=True)  30 us
    psum x1, waiting for transfers between devices, shards(): summed = lax.psum(lax.psum(partial_value, 'pix'), 'sub')  27.1 us
  transfers between devices with their start and end apart: 2, of which 2 were waited for; matrix products, arithmetic and copies ran while one was open for 0% of the time, Pallas kernels for 0%

profile of v1, /device:TPU:0, one launch (start us, length us, event | category | flops | bytes accessed | tf_op | source)
XLA Modules:
  0.0 1170.2 jit_solution(9330474396484308255)
XLA Ops:
  7.2 3.2 copy.48
  10.4 6.3 all-to-all-start
  18.3 47.5 %all-to-all-done = bf16[64,8,2048]{2,0,1:T(8,128)(2,1)S(1)} async-done(((bf16[64,8,2048]{2,0,1:T(8,128)(2,1)}), bf16[64,8,2048]{2,0,1:T(8,128)(2,1)S(1)}, u32[]{:S(2)}, u32[]{:S(2)}) %all-to-all-start) | async-done | bytes 2097184 | tf_op jit(solution)/shard_map/all_to_all | solution.py:45
  65.8 11.0 broadcast_in_dim.86.clone
  76.7 208.3 %while.16 = (s32[]{:T(128)}, bf16[2,32,128,2048]{3,1,0,2:T(8,128)(2,1)}, s32[32]{0:T(128)S(1)}, bf16[512,2048]{1,0:T(8,128)(2,1)S(1)}, f32[32,256]{1,0:T(8,128)S...) while((s32[]{:T(128)}, ...), condition=%wide.region_2.3_spmd, body=%wide.region_1.2_spmd.sunk | while | flops 2168455168 | bytes 52586048 | solution.py:69
  76.8 19.1 %while.17 = (s32[]{:T(128)}, bf16[512,2048]{1,0:T(8,128)(2,1)S(1)}, s32[8,2]{0,1:T(2,128)S(1)}, bf16[8,256,2048]{2,1,0:T(8,128)(2,1)}, s32[]{:T(128)}) while((s32[]{:T(128)}, bf16[512,2048]{1,0:T(8,128)(2,1)S(1)}, s32[8,2]{0,1:T(2,128)S(1)}, bf16[8,256,2048]{2,1,0:T(8,128)(2,1)}, s32[]{:T(128)}) %tuple.54), condition=%wide.while_cond, body=%wide.while_body.sunk | while | flops 2 | bytes 2098265 | solution.py:58
  79.7 1.9 bitcast_dynamic-update-slice_fusion.2
  89.3 1.8 bitcast_dynamic-update-slice_fusion.2
  96.0 12.1 %fusion.53 = bf16[2,8,128,2048]{2,3,0,1:T(8,128)(2,1)} fusion(f32[8]{0:T(128)S(1)} %dynamic_slice.28, bf16[8,256,2048]{2,1,0:T(8,128)(2,1)} %get-tuple-element.242, f32[8,256]{1,0:T(8,128)S(1)} %constant_dynamic-slice_fusion.4, bf16[2,128,256]{2,1,0:T(8,128)(2,1)S(1)} %get-tuple-element.292), kind=kOutput, calls=%fused_computation.6.clone.1 | convolution fusion | flops 2168455168 | bytes 16916512 | tf_op jit(solution)/shard_map/while/body/eval_jaxpr/rkt,btp->rbkp/dot_general | solution.py:62
  108.0 12.6 %copy.50 = bf16[2,8,128,2048]{3,1,0,2:T(8,128)(2,1)} copy(bf16[2,8,128,2048]{2,3,0,1:T(8,128)(2,1)} %fusion.53) | data formatting | bytes 16777216 | tf_op jit(solution)/shard_map/while/body/eval_jaxpr/dynamic_update_slice | solution.py:66
  120.6 8.2 constant_dynamic-update-slice_fusion.2
  128.9 19.1 %while.17 = (s32[]{:T(128)}, bf16[512,2048]{1,0:T(8,128)(2,1)S(1)}, s32[8,2]{0,1:T(2,128)S(1)}, bf16[8,256,2048]{2,1,0:T(8,128)(2,1)}, s32[]{:T(128)}) while((s32[]{:T(128)}, bf16[512,2048]{1,0:T(8,128)(2,1)S(1)}, s32[8,2]{0,1:T(2,128)S(1)}, bf16[8,256,2048]{2,1,0:T(8,128)(2,1)}, s32[]{:T(128)}) %tuple.54), condition=%wide.while_cond, body=%wide.while_body.sunk | while | flops 2 | bytes 2098265 | solution.py:58
  131.8 1.9 bitcast_dynamic-update-slice_fusion.2
  141.3 1.8 bitcast_dynamic-update-slice_fusion.2
  148.0 12.1 %fusion.53 = bf16[2,8,128,2048]{2,3,0,1:T(8,128)(2,1)} fusion(f32[8]{0:T(128)S(1)} %dynamic_slice.28, bf16[8,256,2048]{2,1,0:T(8,128)(2,1)} %get-tuple-element.242, f32[8,256]{1,0:T(8,128)S(1)} %constant_dynamic-slice_fusion.4, bf16[2,128,256]{2,1,0:T(8,128)(2,1)S(1)} %get-tuple-element.292), kind=kOutput, calls=%fused_computation.6.clone.1 | convolution fusion | flops 2168455168 | bytes 16916512 | tf_op jit(solution)/shard_map/while/body/eval_jaxpr/rkt,btp->rbkp/dot_general | solution.py:62
  160.1 12.6 %copy.50 = bf16[2,8,128,2048]{3,1,0,2:T(8,128)(2,1)} copy(bf16[2,8,128,2048]{2,3,0,1:T(8,128)(2,1)} %fusion.53) | data formatting | bytes 16777216 | tf_op jit(solution)/shard_map/while/body/eval_jaxpr/dynamic_update_slice | solution.py:66
  172.6 8.2 constant_dynamic-update-slice_fusion.2
  181.0 19.1 %while.17 = (s32[]{:T(128)}, bf16[512,2048]{1,0:T(8,128)(2,1)S(1)}, s32[8,2]{0,1:T(2,128)S(1)}, bf16[8,256,2048]{2,1,0:T(8,128)(2,1)}, s32[]{:T(128)}) while((s32[]{:T(128)}, bf16[512,2048]{1,0:T(8,128)(2,1)S(1)}, s32[8,2]{0,1:T(2,128)S(1)}, bf16[8,256,2048]{2,1,0:T(8,128)(2,1)}, s32[]{:T(128)}) %tuple.54), condition=%wide.while_cond, body=%wide.while_body.sunk | while | flops 2 | bytes 2098265 | solution.py:58
  183.9 1.9 bitcast_dynamic-update-slice_fusion.2
  200.1 12.1 %fusion.53 = bf16[2,8,128,2048]{2,3,0,1:T(8,128)(2,1)} fusion(f32[8]{0:T(128)S(1)} %dynamic_slice.28, bf16[8,256,2048]{2,1,0:T(8,128)(2,1)} %get-tuple-element.242, f32[8,256]{1,0:T(8,128)S(1)} %constant_dynamic-slice_fusion.4, bf16[2,128,256]{2,1,0:T(8,128)(2,1)S(1)} %get-tuple-element.292), kind=kOutput, calls=%fused_computation.6.clone.1 | convolution fusion | flops 2168455168 | bytes 16916512 | tf_op jit(solution)/shard_map/while/body/eval_jaxpr/rkt,btp->rbkp/dot_general | solution.py:62
  212.2 12.6 %copy.50 = bf16[2,8,128,2048]{3,1,0,2:T(8,128)(2,1)} copy(bf16[2,8,128,2048]{2,3,0,1:T(8,128)(2,1)} %fusion.53) | data formatting | bytes 16777216 | tf_op jit(solution)/shard_map/while/body/eval_jaxpr/dynamic_update_slice | solution.py:66
  224.7 8.2 constant_dynamic-update-slice_fusion.2
  233.0 19.1 %while.17 = (s32[]{:T(128)}, bf16[512,2048]{1,0:T(8,128)(2,1)S(1)}, s32[8,2]{0,1:T(2,128)S(1)}, bf16[8,256,2048]{2,1,0:T(8,128)(2,1)}, s32[]{:T(128)}) while((s32[]{:T(128)}, bf16[512,2048]{1,0:T(8,128)(2,1)S(1)}, s32[8,2]{0,1:T(2,128)S(1)}, bf16[8,256,2048]{2,1,0:T(8,128)(2,1)}, s32[]{:T(128)}) %tuple.54), condition=%wide.while_cond, body=%wide.while_body.sunk | while | flops 2 | bytes 2098265 | solution.py:58
  236.0 1.9 bitcast_dynamic-update-slice_fusion.2
  252.2 12.1 %fusion.53 = bf16[2,8,128,2048]{2,3,0,1:T(8,128)(2,1)} fusion(f32[8]{0:T(128)S(1)} %dynamic_slice.28, bf16[8,256,2048]{2,1,0:T(8,128)(2,1)} %get-tuple-element.242, f32[8,256]{1,0:T(8,128)S(1)} %constant_dynamic-slice_fusion.4, bf16[2,128,256]{2,1,0:T(8,128)(2,1)S(1)} %get-tuple-element.292), kind=kOutput, calls=%fused_computation.6.clone.1 | convolution fusion | flops 2168455168 | bytes 16916512 | tf_op jit(solution)/shard_map/while/body/eval_jaxpr/rkt,btp->rbkp/dot_general | solution.py:62
  264.2 12.6 %copy.50 = bf16[2,8,128,2048]{3,1,0,2:T(8,128)(2,1)} copy(bf16[2,8,128,2048]{2,3,0,1:T(8,128)(2,1)} %fusion.53) | data formatting | bytes 16777216 | tf_op jit(solution)/shard_map/while/body/eval_jaxpr/dynamic_update_slice | solution.py:66
  276.8 8.2 constant_dynamic-update-slice_fusion.2
  285.0 736.0 %all_to_all.34 = bf16[2,32,128,2048]{3,1,0,2:T(8,128)(2,1)} all-to-all(bf16[2,32,128,2048]{3,1,0,2:T(8,128)(2,1)} %get-tuple-element.126), channel_id=1, replica_groups=mesh['group'=2,'tm'=8,'pix'=2,'sub'=1] {'tm'}, dimensions={2} | all-to-all | bytes 67108864 | tf_op jit(solution)/shard_map/all_to_all | solution.py:70
  1021.0 30.0 %copy.21 = bf16[2,32,16,8,2048]{4,3,1,0,2:T(8,128)(2,1)} copy(bf16[2,32,16,8,2048]{4,1,0,2,3:T(8,128)(2,1)} %bitcast.107) | data formatting | bytes 67108864 | tf_op jit(solution)/shard_map/all_to_all | solution.py:70
  1051.0 49.9 %reshape.182 = bf16[64,16,16384]{2,0,1:T(8,128)(2,1)} reshape(bf16[2,32,16,8,2048]{4,3,1,0,2:T(8,128)(2,1)} %copy.21) | data formatting | bytes 67108864 | tf_op jit(solution)/shard_map/reshape | solution.py:40
  1100.9 23.5 %fusion.16 = f32[16,64,64]{2,1,0:T(8,128)} fusion(bf16[64,16,16384]{2,0,1:T(8,128)(2,1)} %reshape.182), kind=kOutput, calls=%fused_computation.64 | convolution fusion | flops 2147483648 | bytes 33816576 | tf_op jit(solution)/shard_map/ifp,jfp->fij/dot_general | solution.py:41
  1124.4 27.1 %all-reduce.3.cloned.1.call-done = f32[16,64,64]{2,1,0:T(8,128)} async-done(((f32[16,64,64]{2,1,0:T(8,128)}), f32[16,64,64]{2,1,0:T(8,128)}) %all-reduce.3.cloned.1.call-update) | async-done | bytes 262160 | tf_op jit(solution)/shard_map/psum | solution.py:72
  (160 shorter events, 79.1 us)
Async XLA Ops:
  10.4 55.4 %all-to-all-start = ((bf16[64,8,2048]{2,0,1:T(8,128)(2,1)}), bf16[64,8,2048]{2,0,1:T(8,128)(2,1)S(1)}, u32[]{:S(2)}, u32[]{:S(2)}) async-start(bf16[64,8,2048]{2,0,1:T(8,128)(2,1)} %bitcast.108), calls=%async_computation | async-start | bytes 4194304 | tf_op jit(solution)/shard_map/all_to_all | solution.py:45
  16.7 1134.8 %all-reduce.3.cloned.1.call-start = ((), (), s32[]{:S(2)}) async-start(), calls=%async_computation.2 | async-start | bytes 1048576 | tf_op jit(solution)/shard_map/psum | solution.py:72
  65.7 11.0 copy-start.1
  1152.6 10.8 copy-start
Sparse Core Ops, SparseCore 0:
  1124.5 26.9 all-reduce.2
